TPU v7x, 128 devices: a whole 4x4x4 slice. The times are simulated.
128 devices in a mesh: seq: 8 (over x, z_hi), role: 2 (over z_lo), exp: 8 (over y, core).
Axes of the slice: x: 4, y: 4, z: 4 (z_hi: 2, z_lo: 2; z = z_hi * 2 + z_lo), core: 2. Of those that a mesh axis runs over, the one named last changes fastest.
Arguments:
- tokens: bfloat16 [2, 65536, 768], P(None, ('seq', 'role', 'exp')), may hold values from -6 to 6
- expert_ids: int32 [2, 65536, 1], P(None, ('seq', 'role', 'exp')), may hold values from 0 to 127; in each aligned block of 512 rows (0 to 511, 512 to 1023, ..., all dimensions but the last counted through in order) at most 8 rows name the same one
- attn_qkv: bfloat16 [768, 2304], P(('seq', 'role')), may hold values from -0.21875 to 0.21875
- attn_out: bfloat16 [768, 768], P(('seq', 'role')), may hold values from -0.21875 to 0.21875
- norm_attn: float32 [768], replicated, may hold values from 0.1 to 1.9
- norm_ffn: float32 [768], replicated, may hold values from 0.1 to 1.9
- router: bfloat16 [768, 128], replicated, may hold values from -0.43164062 to 0.43164062
- expert_in: bfloat16 [128, 768, 3072], P(('seq', 'role', 'exp')), may hold values from -0.21875 to 0.21875
- expert_out: bfloat16 [128, 3072, 768], P(('seq', 'role', 'exp')), may hold values from -0.109375 to 0.109375
Outputs:
- layer_out: bfloat16 [2, 65536, 768], P(None, ('seq', 'role', 'exp'))
Inputs may be any that keep to these rules, and one draw needn't show every extreme that they name: `expert_ids`: in each micro-batch the 512 tokens of one device name any one expert at most 8 times.
All inputs are finite; a program needn't handle non-finite values.
Results may differ from a plain program's by a relative error of at most 0.0058.
Values may be sent and summed in bfloat16 or wider, within the bound.
No kernel may reach another device: no remote copies, remote signals or barrier semaphores. Data moves between devices by JAX's collectives and lax.ppermute only.
A program may use at most 128 MiB of HBM per device.

v0:
```python
import jax
import jax.numpy as jnp
from jax import lax
from jax.sharding import PartitionSpec as P

HEADS = 12
LEN = 512


def scale_rows(values, gain_vec):
    floats = values.astype(jnp.float32)
    return floats * lax.rsqrt(jnp.mean(floats * floats, -1, keepdims=True) + 1e-06) * gain_vec


def add_columns(source, weight_piece):
    return jnp.dot(source, weight_piece, preferred_element_type=jnp.float32)


def body(
    tokens, expert_ids, attn_qkv, attn_out, norm_attn, norm_ffn, router, expert_in, expert_out
):
    batch_count, row_count, model_width = tokens.shape
    token_count = batch_count * row_count
    head_dim = model_width // HEADS
    flat_tokens = tokens.reshape(token_count, model_width)
    normed = scale_rows(flat_tokens, norm_attn).astype(jnp.bfloat16)
    projected = add_columns(
        normed, lax.all_gather(attn_qkv, ("seq", "role"), axis=0, tiled=True)
    ).astype(jnp.bfloat16)
    heads_split = projected.reshape(token_count // LEN, LEN, 3, HEADS, head_dim)

    def attend(sequence):
        scores = jnp.einsum(
            "qhd,khd->hqk", sequence[:, 0], sequence[:, 1], preferred_element_type=jnp.float32
        ) * head_dim ** (-0.5)
        weights = jnp.exp(scores)
        weights_norm = (weights / jnp.sum(weights, -1, keepdims=True)).astype(jnp.bfloat16)
        return jnp.einsum(
            "hqk,khd->qhd", weights_norm, sequence[:, 2], preferred_element_type=jnp.float32
        ).astype(jnp.bfloat16)

    context = lax.map(attend, heads_split).reshape(token_count, model_width)
    mixed = add_columns(context, lax.all_gather(attn_out, ("seq", "role"), axis=0, tiled=True))
    attended = (flat_tokens.astype(jnp.float32) + mixed).astype(jnp.bfloat16)
    normed_ffn = scale_rows(attended, norm_ffn).astype(jnp.bfloat16)
    experts = lax.axis_size(("seq", "role", "exp"))
    capacity = max(2, 2 * row_count // experts)
    chosen_ids = expert_ids.reshape(token_count)
    logits = jnp.dot(normed_ffn, router, preferred_element_type=jnp.float32)
    picked = chosen_ids[:, None] == lax.broadcasted_iota(jnp.int32, (1, experts), 1)
    gate_value = jax.nn.sigmoid(jnp.sum(jnp.where(picked, logits, 0.0), -1))
    marked = picked.reshape(batch_count, row_count, experts)
    triangle = (
        lax.broadcasted_iota(jnp.int32, (row_count, row_count), 0)
        >= lax.broadcasted_iota(jnp.int32, (row_count, row_count), 1)
    ).astype(jnp.bfloat16)
    running = jnp.einsum(
        "ij,bje->bie", triangle, marked.astype(jnp.bfloat16), preferred_element_type=jnp.float32
    )
    slot_index = jnp.sum(jnp.where(marked, running, 0.0), -1).astype(jnp.int32) - 1
    batch_index = lax.broadcasted_iota(jnp.int32, (batch_count, 1), 0)
    position = (
        chosen_ids.reshape(batch_count, row_count) * (batch_count * capacity)
        + batch_index * capacity
        + slot_index
    ).reshape(token_count)
    slots_total = experts * batch_count * capacity
    outgoing = jnp.zeros((slots_total, model_width), jnp.bfloat16).at[position].set(normed_ffn)
    outgoing = outgoing.reshape(experts, batch_count, capacity, model_width)
    weight_in = expert_in[0]
    weight_out = expert_out[0]
    rows_in = lax.all_to_all(
        outgoing, ("seq", "role", "exp"), split_axis=0, concat_axis=0, tiled=True
    )
    old_shape = rows_in.shape
    hidden = jax.nn.relu(
        jnp.dot(rows_in.reshape(-1, model_width), weight_in, preferred_element_type=jnp.float32)
    ).astype(jnp.bfloat16)
    returned_rows = lax.all_to_all(
        jnp.dot(hidden, weight_out, preferred_element_type=jnp.float32)
        .astype(jnp.bfloat16)
        .reshape(old_shape),
        ("seq", "role", "exp"),
        split_axis=0,
        concat_axis=0,
        tiled=True,
    )
    returned_rows = returned_rows.reshape(slots_total, model_width)
    result = returned_rows[position]
    layer_out = (
        attended.astype(jnp.float32) + gate_value[:, None] * result.astype(jnp.float32)
    ).astype(jnp.bfloat16)
    return layer_out.reshape(batch_count, row_count, model_width)


def solution(mesh):
    in_specs = (
        P(None, ("seq", "role", "exp"), None),
        P(None, ("seq", "role", "exp"), None),
        P(("seq", "role"), None),
        P(("seq", "role"), None),
        P(),
        P(),
        P(),
        P(("seq", "role", "exp"), None, None),
        P(("seq", "role", "exp"), None, None),
    )
    out_specs = P(None, ("seq", "role", "exp"), None)
    return jax.shard_map(body, mesh=mesh, in_specs=in_specs, out_specs=out_specs, check_vma=False)
```

profile of v0, /device:TPU:1, one launch (start us, length us, event | category | flops | bytes accessed | tf_op | source)
XLA Modules:
  0.0 254.4 jit_solution(380767495640874659)
XLA Ops:
  6.5 0.0 copy-start
  6.5 0.0 copy-start.1
  6.5 0.0 copy-start.3
  6.5 0.0 all-gather.3.cloned.1.call-start
  6.5 0.7 all-gather.3.cloned.1.call-update
  7.3 0.0 all-gather.5.cloned.1.call-start
  7.3 0.7 all-gather.5.cloned.1.call-update
  8.0 0.7 copy.23
  8.7 0.7 broadcast_multiply_fusion
  9.4 1.8 fusion.20
  11.2 0.4 fusion.28
  11.6 0.1 broadcast_bitcast_fusion
  11.7 0.0 copy-done.1
  11.7 0.0 copy-done.3
  11.7 1.6 fusion.22
  13.3 48.2 %all-gather.3.cloned.1.call-done = bf16[768,2304]{1,0:T(8,128)(2,1)} async-done(((bf16[48,2304]{1,0:T(8,128)(2,1)}), bf16[768,2304]{1,0:T(8,128)(2,1)}) %all-gather.3.cloned.1.call-update) | async-done | bytes 3538960 | tf_op jit(solution)/shard_map/all_gather | solution.py:28
  61.5 8.4 %convolution_convert_fusion = bf16[1024,2304]{1,0:T(8,128)(2,1)} fusion(bf16[1024,768]{1,0:T(8,128)(2,1)} %fusion.22, bf16[768,2304]{1,0:T(8,128)(2,1)} %all-gather.3.cloned.1.call-done), kind=kOutput, calls=%fused_computation.16 | convolution fusion | flops 3626237952 | bytes 9830400 | tf_op jit(solution)/shard_map/dot_general | solution.py:16
  69.9 6.7 %copy.13 = bf16[1024,2304]{0,1:T(8,128)(2,1)} copy(bf16[1024,2304]{1,0:T(8,128)(2,1)} %convolution_convert_fusion) | data formatting | bytes 9437184 | tf_op jit(solution)/shard_map/convert_element_type | solution.py:29
  76.6 8.8 %reshape.127 = bf16[2,512,3,12,64]{1,0,4,3,2:T(2,128)(2,1)} reshape(bf16[1024,2304]{0,1:T(8,128)(2,1)} %copy.13) | data formatting | bytes 9437184 | tf_op jit(solution)/shard_map/reshape | solution.py:30
  85.5 5.5 %copy.14 = bf16[2,512,3,12,64]{1,4,3,2,0:T(8,128)(2,1)} copy(bf16[2,512,3,12,64]{1,0,4,3,2:T(2,128)(2,1)} %reshape.127) | data formatting | bytes 9437184 | tf_op jit(solution)/shard_map/while | solution.py:42
  91.0 13.4 %while.10 = (s32[]{:T(128)}, bf16[2,512,12,64]{1,3,2,0:T(8,128)(2,1)S(1)}, bf16[2,512,3,12,64]{1,4,3,2,0:T(8,128)(2,1)}, s32[]{:T(128)}) while((s32[]{:T(128)}, bf16[2,512,12,64]{1,3,2,0:T(8,128)(2,1)S(1)}, bf16[2,512,3,12,64]{1,4,3,2,0:T(8,128)(2,1)}, s32[]{:T(128)}) %tuple.24), condition=%wide.region_3.4_spmd, body=%wide.region_1.3_spmd.sunk | while | flops 821422080 | bytes 33087548 | solution.py:42
  91.0 1.9 dynamic-slice_bitcast_fusion.2
  92.9 2.3 fusion.43
  95.2 2.4 fusion.44
  97.7 1.9 dynamic-slice_bitcast_fusion.2
  99.6 2.3 fusion.43
  102.0 2.4 fusion.44
  104.4 1.6 copy.15
  106.0 0.4 copy.19
  106.4 0.0 all-gather.5.cloned.1.call-done
  106.5 0.0 copy-start.4
  106.5 4.0 %fusion.16 = (f32[1024]{0:T(1024)S(1)}, bf16[1024,768]{1,0:T(8,128)(2,1)}) fusion(bf16[1024,768]{0,1:T(8,128)(2,1)S(1)} %bitcast.102, bf16[768,768]{1,0:T(8,128)(2,1)} %all-gather.5.cloned.1.call-done, bf16[2,512,768]{2,1,0:T(8,128)(2,1)S(1)} %copy-done.1), kind=kOutput, calls=%fused_computation.24 | convolution fusion | flops 1212677120 | bytes 5902336 | tf_op jit(solution)/shard_map/dot_general | solution.py:16
  110.5 0.0 copy-done.4
  110.5 7.2 %scatter_custom_fusion = bf16[2048,768]{1,0:T(8,128)(2,1)S(1)} fusion(s32[1024]{0:T(1024)S(1)} %bitcast.105, bf16[]{:T(256)} %constant.7.clone.1, bf16[1024,768]{1,0:T(8,128)(2,1)} %get-tuple-element.38, f32[768]{0:T(1024)S(1)} %copy-done.4, f32[1024]{0:T(1024)S(1)} %add_rsqrt_fusion), kind=kCustom, calls=%fused_computation.35 | custom fusion | flops 3145728 | bytes 4726786 | tf_op jit(solution)/shard_map/scatter | solution.py:68
  117.7 49.2 %all_to_all.10 = bf16[128,2,8,768]{3,2,1,0:T(8,128)(2,1)} all-to-all(bf16[128,2,8,768]{3,2,1,0:T(8,128)(2,1)S(1)} %bitcast.98), channel_id=1, replica_groups=mesh['seq'=8,'role'=2,'exp'=8] {'seq','role','exp'}, dimensions={0} | all-to-all | bytes 6291456 | tf_op jit(solution)/shard_map/all_to_all | solution.py:72
  166.9 25.4 %fusion.11 = bf16[2048,768]{1,0:T(8,128)(2,1)} fusion(bf16[1,3072,768]{2,1,0:T(8,128)(2,1)} %param.19, bf16[2048,768]{1,0:T(8,128)(2,1)} %bitcast.101, bf16[1,768,3072]{2,1,0:T(8,128)(2,1)} %param.18), kind=kOutput, calls=%fused_computation.23 | convolution fusion | flops 19341508608 | bytes 15728640 | tf_op jit(solution)/shard_map/dot_general | solution.py:80
  192.3 0.0 copy-start.2
  192.3 4.8 %all-to-all-start.1 = ((bf16[128,2,8,768]{3,2,1,0:T(8,128)(2,1)}), bf16[128,2,8,768]{3,2,1,0:T(8,128)(2,1)S(1)}, u32[]{:S(2)}, u32[]{:S(2)}) async-start(bf16[128,2,8,768]{3,2,1,0:T(8,128)(2,1)} %bitcast.100), calls=%async_computation.1 | async-start | bytes 6291456 | tf_op jit(solution)/shard_map/all_to_all | solution.py:79
  197.1 0.0 copy-done
  197.1 0.0 copy-done.2
  197.1 2.2 fusion.27
  199.3 39.5 %all-to-all-done.1 = bf16[128,2,8,768]{3,2,1,0:T(8,128)(2,1)S(1)} async-done(((bf16[128,2,8,768]{3,2,1,0:T(8,128)(2,1)}), bf16[128,2,8,768]{3,2,1,0:T(8,128)(2,1)S(1)}, u32[]{:S(2)}, u32[]{:S(2)}) %all-to-all-start.1) | async-done | bytes 3145760 | tf_op jit(solution)/shard_map/all_to_all | solution.py:79
  238.8 5.2 %gather_fusion = bf16[1024,768]{1,0:T(8,128)(2,1)} fusion(bf16[2048,768]{1,0:T(8,128)(2,1)S(1)} %bitcast.97, s32[1024]{0:T(1024)S(1)} %broadcast_clamp_fusion), kind=kCustom, calls=%fused_computation | custom fusion | bytes 3149824 | tf_op jit(solution)/shard_map/gather | solution.py:89
  244.0 3.5 %fusion.19 = bf16[1024,768]{1,0:T(8,128)(2,1)} fusion(bf16[1024,768]{1,0:T(8,128)(2,1)} %get-tuple-element.38, bf16[1024,768]{1,0:T(8,128)(2,1)} %gather_fusion, f32[1024]{0:T(1024)S(1)} %add_divide_fusion), kind=kLoop, calls=%fused_computation.27 | loop fusion | flops 3932160 | bytes 4722688 | tf_op jit(solution)/shard_map/convert_element_type | solution.py:92
  (11 shorter events, 0.1 us)
Async XLA Ops:
  6.5 190.6 %copy-start = (bf16[768,128]{1,0:T(8,128)(2,1)S(1)}, bf16[768,128]{1,0:T(8,128)(2,1)}, u32[]{:S(2)}) copy-start(bf16[768,128]{1,0:T(8,128)(2,1)} %param.17) | copy-start | bytes 589828
  6.5 5.2 %copy-start.1 = (bf16[2,512,768]{2,1,0:T(8,128)(2,1)S(1)}, bf16[2,512,768]{2,1,0:T(8,128)(2,1)}, u32[]{:S(2)}) copy-start(bf16[2,512,768]{2,1,0:T(8,128)(2,1)} %param.11) | copy-start | bytes 4718596
  6.5 5.2 %copy-start.3 = (f32[768]{0:T(1024)S(1)}, f32[768]{0:T(1024)}, u32[]{:S(2)}) copy-start(f32[768]{0:T(1024)} %param.15) | copy-start | bytes 9220
  6.5 55.0 %all-gather.3.cloned.1.call-start = ((), (), s32[]{:S(2)}) async-start(), calls=%async_computation.2 | async-start | bytes 3760128 | tf_op jit(solution)/shard_map/all_gather | solution.py:28
  7.3 99.2 %all-gather.5.cloned.1.call-start = ((), (), s32[]{:S(2)}) async-start(), calls=%async_computation.3 | async-start | bytes 1253376 | tf_op jit(solution)/shard_map/all_gather | solution.py:43
  106.5 4.0 %copy-start.4 = (f32[768]{0:T(1024)S(1)}, f32[768]{0:T(1024)}, u32[]{:S(2)}) copy-start(f32[768]{0:T(1024)} %param.16) | copy-start | bytes 9220
  192.3 4.8 %copy-start.2 = (s32[2,512,1]{1,2,0:T(1,128)S(1)}, s32[2,512,1]{1,2,0:T(1,128)}, u32[]{:S(2)}) copy-start(s32[2,512,1]{1,2,0:T(1,128)} %param.12) | copy-start | bytes 12292
  192.3 46.5 %all-to-all-start.1 = ((bf16[128,2,8,768]{3,2,1,0:T(8,128)(2,1)}), bf16[128,2,8,768]{3,2,1,0:T(8,128)(2,1)S(1)}, u32[]{:S(2)}, u32[]{:S(2)}) async-start(bf16[128,2,8,768]{3,2,1,0:T(8,128)(2,1)} %bitcast.100), calls=%async_computation.1 | async-start | bytes 6291456 | tf_op jit(solution)/shard_map/all_to_all | solution.py:79
Sparse Core Ops, SparseCore 0:
  9.5 51.9 all-gather.2
  63.7 40.5 all-gather.4
where the time goes:
time: 255 us; the launch traced here: 254 us
  waiting for transfers between devices  89.1 us (35%)
  matrix products  49.9 us (20%)
  blocking collectives  49.2 us (19%)
  local copies, waits for them, and re-layouts  33 us (13%)
  other arithmetic  14.9 us (6%)
  between operations  13.6 us (5%)
  starting transfers between devices  4.79 us (2%)
    all_to_all x1, blocking collectives, body(): lax.all_to_all(outgoing, ('seq', 'role', 'exp'), split_axis=0, concat_axi...  49.2 us
    all_gather x1, waiting for transfers between devices, body(): lax.all_gather(attn_qkv, ('seq', 'role'), axis=0, tiled=True)  48.2 us
    all_to_all x1, waiting for transfers between devices, body(): lax.all_to_all(jnp.dot(hidden, weight_out, preferred_element_type=jnp.flo...  39.5 us
    dot_general x1, matrix products, body(): jnp.dot(hidden, weight_out, preferred_element_type=jnp.float32)  25.4 us
    dot_general x2, matrix products, add_columns(): return jnp.dot(source, weight_piece, preferred_element_type=jnp.float32)  12.4 us
    reshape x1, local copies, waits for them, and re-layouts, body(): heads_split = projected.reshape(token_count // LEN, LEN, 3, HEADS, head_dim)  8.81 us
    scatter x1, other arithmetic, body(): jnp.zeros((slots_total, model_width), jnp.bfloat16).at[position]  7.21 us
    while x2, local copies, waits for them, and re-layouts, body(): context = lax.map(attend, heads_split).reshape(token_count, model_width)  7.17 us
  transfers between devices with their start and end apart: 3, of which 2 were waited for; matrix products, arithmetic and copies ran while one was open for 21% of the time, Pallas kernels for 0%

commit v1 on v0

--- a/solution.py
+++ b/solution.py
@@ -25,7 +25,13 @@
     flat_tokens = tokens.reshape(token_count, model_width)
     normed = scale_rows(flat_tokens, norm_attn).astype(jnp.bfloat16)
     projected = add_columns(
-        normed, lax.all_gather(attn_qkv, ("seq", "role"), axis=0, tiled=True)
+        normed,
+        jnp.concatenate(
+            lax.all_to_all(
+                jnp.stack([attn_qkv] * lax.axis_size(("seq", "role"))), ("seq", "role"), 0, 0
+            ),
+            axis=0,
+        ),
     ).astype(jnp.bfloat16)
     heads_split = projected.reshape(token_count // LEN, LEN, 3, HEADS, head_dim)
 

time: 255 us -> 265 us (1.039)
  starting transfers between devices: 4.79 us -> 13.4 us
  blocking collectives: 49.2 us -> 56.3 us
  waiting for transfers between devices: 89.1 us -> 83.3 us
    all_gather x1 -> x0, waiting for transfers between devices: 48.2 us -> none  [body(): lax.all_gather(attn_qkv, ('seq', 'role'), axis=0, tiled=True)]
    all_to_all x0 -> x1, waiting for transfers between devices: none -> 43.1 us  [body(): lax.all_to_all(jnp.stack([attn_qkv] * lax.axis_size(('seq', 'role'))), ('...]
    all_to_all x0 -> x1, starting transfers between devices: none -> 8.59 us  [body(): lax.all_to_all(jnp.stack([attn_qkv] * lax.axis_size(('seq', 'role'))), ('...]
    all_to_all x1, blocking collectives: 49.2 us -> 56.3 us  [body(): lax.all_to_all(outgoing, ('seq', 'role', 'exp'), split_axis=0, concat_axi...]
    another operation x0 -> x1, local copies, waits for them, and re-layouts: none -> 2.96 us  [body(): jnp.stack([attn_qkv] * lax.axis_size(('seq', 'role')))]
  transfers between devices with their start and end apart: 3 -> 3, of which waited for: 2 -> 2; matrix products, arithmetic and copies ran while one was open for 21% -> 19% of each run, Pallas kernels for 0% -> 0%
where the time goes in v1:
time: 265 us; the launch traced here: 264 us
  waiting for transfers between devices  83.3 us (31%)
  blocking collectives  56.3 us (21%)
  matrix products  49.8 us (19%)
  local copies, waits for them, and re-layouts  35.2 us (13%)
  between operations  13.6 us (5%)
  starting transfers between devices  13.4 us (5%)
  other arithmetic  12.8 us (5%)
    all_to_all x1, blocking collectives, body(): lax.all_to_all(outgoing, ('seq', 'role', 'exp'), split_axis=0, concat_axi...  56.3 us
    all_to_all x1, waiting for transfers between devices, body(): lax.all_to_all(jnp.stack([attn_qkv] * lax.axis_size(('seq', 'role'))), ('...  43.1 us
    all_to_all x1, waiting for transfers between devices, body(): lax.all_to_all(jnp.dot(hidden, weight_out, preferred_element_type=jnp.flo...  39.5 us
    dot_general x1, matrix products, body(): jnp.dot(hidden, weight_out, preferred_element_type=jnp.float32)  25.4 us
    dot_general x2, matrix products, add_columns(): return jnp.dot(source, weight_piece, preferred_element_type=jnp.float32)  12.4 us
    reshape x1, local copies, waits for them, and re-layouts, body(): heads_split = projected.reshape(token_count // LEN, LEN, 3, HEADS, head_dim)  8.82 us
    all_to_all x1, starting transfers between devices, body(): lax.all_to_all(jnp.stack([attn_qkv] * lax.axis_size(('seq', 'role'))), ('...  8.59 us
    scatter x1, other arithmetic, body(): jnp.zeros((slots_total, model_width), jnp.bfloat16).at[position]  7.21 us
  transfers between devices with their start and end apart: 3, of which 2 were waited for; matrix products, arithmetic and copies ran while one was open for 19% of the time, Pallas kernels for 0%

profile of v1, /device:TPU:1, one launch (start us, length us, event | category | flops | bytes accessed | tf_op | source)
XLA Modules:
  0.0 264.5 jit_solution(7236456382387600161)
XLA Ops:
  6.5 0.0 copy-start
  6.5 3.0 %stack.2 = bf16[16,48,2304]{2,1,0:T(8,128)(2,1)} broadcast(bf16[48,2304]{1,0:T(8,128)(2,1)} %param.13), dimensions={1,2} | broadcast | bytes 3760128 | tf_op jit(solution)/shard_map/stack | solution.py:31
  9.5 0.0 copy-start.2
  9.5 0.0 copy-start.1
  9.5 0.0 copy-start.4
  9.5 8.6 %all-to-all-start = ((bf16[16,48,2304]{2,1,0:T(8,128)(2,1)}), bf16[16,48,2304]{2,1,0:T(8,128)(2,1)}, u32[]{:S(2)}, u32[]{:S(2)}) async-start(bf16[16,48,2304]{2,1,0:T(8,128)(2,1)} %stack.2), calls=%async_computation | async-start | bytes 7077888 | tf_op jit(solution)/shard_map/all_to_all | solution.py:30
  18.1 0.0 all-gather.2.cloned.1.call-start
  18.2 0.7 all-gather.2.cloned.1.call-update
  18.9 0.0 copy-done.2
  18.9 0.4 fusion.25
  19.3 0.1 broadcast_bitcast_fusion
  19.4 0.0 copy-done.1
  19.4 0.4 multiply_reduce_fusion
  19.8 0.0 copy-done.4
  19.8 1.6 multiply_convert_fusion
  21.4 43.1 %all-to-all-done = bf16[16,48,2304]{2,1,0:T(8,128)(2,1)} async-done(((bf16[16,48,2304]{2,1,0:T(8,128)(2,1)}), bf16[16,48,2304]{2,1,0:T(8,128)(2,1)}, u32[]{:S(2)}, u32[]{:S(2)}) %all-to-all-start) | async-done | bytes 3538976 | tf_op jit(solution)/shard_map/all_to_all | solution.py:30
  64.5 8.4 %convolution_convert_fusion = bf16[1024,2304]{1,0:T(8,128)(2,1)} fusion(bf16[1024,768]{1,0:T(8,128)(2,1)} %bitcast.96, bf16[768,2304]{1,0:T(8,128)(2,1)} %bitcast.8), kind=kOutput, calls=%fused_computation.16 | convolution fusion | flops 3626237952 | bytes 9830400 | tf_op jit(solution)/shard_map/dot_general | solution.py:16
  72.9 6.7 %copy.13 = bf16[1024,2304]{0,1:T(8,128)(2,1)} copy(bf16[1024,2304]{1,0:T(8,128)(2,1)} %convolution_convert_fusion) | data formatting | bytes 9437184 | tf_op jit(solution)/shard_map/convert_element_type | solution.py:35
  79.6 8.8 %reshape.138 = bf16[2,512,3,12,64]{1,0,4,3,2:T(2,128)(2,1)} reshape(bf16[1024,2304]{0,1:T(8,128)(2,1)} %copy.13) | data formatting | bytes 9437184 | tf_op jit(solution)/shard_map/reshape | solution.py:36
  88.4 5.5 %copy.14 = bf16[2,512,3,12,64]{1,4,3,2,0:T(8,128)(2,1)} copy(bf16[2,512,3,12,64]{1,0,4,3,2:T(2,128)(2,1)} %reshape.138) | data formatting | bytes 9437184 | tf_op jit(solution)/shard_map/while | solution.py:48
  94.0 13.4 %while.10 = (s32[]{:T(128)}, bf16[2,512,12,64]{1,3,2,0:T(8,128)(2,1)S(1)}, bf16[2,512,3,12,64]{1,4,3,2,0:T(8,128)(2,1)}, s32[]{:T(128)}) while((s32[]{:T(128)}, bf16[2,512,12,64]{1,3,2,0:T(8,128)(2,1)S(1)}, bf16[2,512,3,12,64]{1,4,3,2,0:T(8,128)(2,1)}, s32[]{:T(128)}) %tuple.24), condition=%wide.region_3.4_spmd, body=%wide.region_1.3_spmd.sunk | while | flops 821422080 | bytes 33087548 | solution.py:48
  94.0 1.9 dynamic-slice_bitcast_fusion.2
  95.9 2.3 fusion.40
  98.2 2.4 fusion.41
  100.6 1.9 dynamic-slice_bitcast_fusion.2
  102.6 2.3 fusion.40
  104.9 2.4 fusion.41
  107.3 1.6 copy.15
  109.0 0.4 copy.18
  109.4 0.0 all-gather.2.cloned.1.call-done
  109.4 0.0 copy-start.5
  109.4 4.0 %fusion.16 = (f32[1024]{0:T(1024)S(1)}, bf16[1024,768]{1,0:T(8,128)(2,1)}) fusion(bf16[1024,768]{0,1:T(8,128)(2,1)S(1)} %bitcast.97, bf16[768,768]{1,0:T(8,128)(2,1)} %all-gather.2.cloned.1.call-done, bf16[2,512,768]{2,1,0:T(8,128)(2,1)S(1)} %copy-done.1), kind=kOutput, calls=%fused_computation.24 | convolution fusion | flops 1212677120 | bytes 5902336 | tf_op jit(solution)/shard_map/dot_general | solution.py:16
  113.4 0.0 copy-done.5
  113.4 7.2 %scatter_custom_fusion = bf16[2048,768]{1,0:T(8,128)(2,1)S(1)} fusion(s32[1024]{0:T(1024)S(1)} %bitcast.99, bf16[]{:T(256)} %constant.7.clone.1, bf16[1024,768]{1,0:T(8,128)(2,1)} %get-tuple-element.38, f32[768]{0:T(1024)S(1)} %copy-done.5, f32[1024]{0:T(1024)S(1)} %add_rsqrt_fusion), kind=kCustom, calls=%fused_computation.32 | custom fusion | flops 3145728 | bytes 4726786 | tf_op jit(solution)/shard_map/scatter | solution.py:74
  120.6 56.3 %all_to_all.15 = bf16[128,2,8,768]{3,2,1,0:T(8,128)(2,1)} all-to-all(bf16[128,2,8,768]{3,2,1,0:T(8,128)(2,1)S(1)} %bitcast.92), channel_id=1, replica_groups=mesh['seq'=8,'role'=2,'exp'=8] {'seq','role','exp'}, dimensions={0} | all-to-all | bytes 6291456 | tf_op jit(solution)/shard_map/all_to_all | solution.py:78
  176.9 25.4 %fusion.11 = bf16[2048,768]{1,0:T(8,128)(2,1)} fusion(bf16[1,3072,768]{2,1,0:T(8,128)(2,1)} %param.19, bf16[2048,768]{1,0:T(8,128)(2,1)} %bitcast.95, bf16[1,768,3072]{2,1,0:T(8,128)(2,1)} %param.18), kind=kOutput, calls=%fused_computation.23 | convolution fusion | flops 19341508608 | bytes 15728640 | tf_op jit(solution)/shard_map/dot_general | solution.py:86
  202.4 0.0 copy-start.3
  202.4 4.8 %all-to-all-start.2 = ((bf16[128,2,8,768]{3,2,1,0:T(8,128)(2,1)}), bf16[128,2,8,768]{3,2,1,0:T(8,128)(2,1)S(1)}, u32[]{:S(2)}, u32[]{:S(2)}) async-start(bf16[128,2,8,768]{3,2,1,0:T(8,128)(2,1)} %bitcast.94), calls=%async_computation.2 | async-start | bytes 6291456 | tf_op jit(solution)/shard_map/all_to_all | solution.py:85
  207.1 0.0 copy-done
  207.2 0.0 copy-done.3
  207.2 2.2 fusion.24
  209.3 39.5 %all-to-all-done.2 = bf16[128,2,8,768]{3,2,1,0:T(8,128)(2,1)S(1)} async-done(((bf16[128,2,8,768]{3,2,1,0:T(8,128)(2,1)}), bf16[128,2,8,768]{3,2,1,0:T(8,128)(2,1)S(1)}, u32[]{:S(2)}, u32[]{:S(2)}) %all-to-all-start.2) | async-done | bytes 3145760 | tf_op jit(solution)/shard_map/all_to_all | solution.py:85
  248.9 5.2 %gather_fusion = bf16[1024,768]{1,0:T(8,128)(2,1)} fusion(bf16[2048,768]{1,0:T(8,128)(2,1)S(1)} %bitcast.91, s32[1024]{0:T(1024)S(1)} %broadcast_clamp_fusion), kind=kCustom, calls=%fused_computation | custom fusion | bytes 3149824 | tf_op jit(solution)/shard_map/gather | solution.py:95
  254.1 3.5 %fusion.19 = bf16[1024,768]{1,0:T(8,128)(2,1)} fusion(bf16[1024,768]{1,0:T(8,128)(2,1)} %get-tuple-element.38, bf16[1024,768]{1,0:T(8,128)(2,1)} %gather_fusion, f32[1024]{0:T(1024)S(1)} %add_divide_fusion), kind=kLoop, calls=%fused_computation.27 | loop fusion | flops 3932160 | bytes 4722688 | tf_op jit(solution)/shard_map/convert_element_type | solution.py:98
  (12 shorter events, 0.1 us)
Async XLA Ops:
  6.5 200.6 %copy-start = (bf16[768,128]{1,0:T(8,128)(2,1)S(1)}, bf16[768,128]{1,0:T(8,128)(2,1)}, u32[]{:S(2)}) copy-start(bf16[768,128]{1,0:T(8,128)(2,1)} %param.17) | copy-start | bytes 589828
  9.5 9.4 %copy-start.2 = (s32[2,512,1]{1,2,0:T(1,128)S(1)}, s32[2,512,1]{1,2,0:T(1,128)}, u32[]{:S(2)}) copy-start(s32[2,512,1]{1,2,0:T(1,128)} %param.12) | copy-start | bytes 12292
  9.5 9.9 %copy-start.1 = (bf16[2,512,768]{2,1,0:T(8,128)(2,1)S(1)}, bf16[2,512,768]{2,1,0:T(8,128)(2,1)}, u32[]{:S(2)}) copy-start(bf16[2,512,768]{2,1,0:T(8,128)(2,1)} %param.11) | copy-start | bytes 4718596
  9.5 10.3 %copy-start.4 = (f32[768]{0:T(1024)S(1)}, f32[768]{0:T(1024)}, u32[]{:S(2)}) copy-start(f32[768]{0:T(1024)} %param.15) | copy-start | bytes 9220
  9.5 55.0 %all-to-all-start = ((bf16[16,48,2304]{2,1,0:T(8,128)(2,1)}), bf16[16,48,2304]{2,1,0:T(8,128)(2,1)}, u32[]{:S(2)}, u32[]{:S(2)}) async-start(bf16[16,48,2304]{2,1,0:T(8,128)(2,1)} %stack.2), calls=%async_computation | async-start | bytes 7077888 | tf_op jit(solution)/shard_map/all_to_all | solution.py:30
  18.1 91.3 %all-gather.2.cloned.1.call-start = ((), (), s32[]{:S(2)}) async-start(), calls=%async_computation.3 | async-start | bytes 1253376 | tf_op jit(solution)/shard_map/all_gather | solution.py:49
  109.4 4.0 %copy-start.5 = (f32[768]{0:T(1024)S(1)}, f32[768]{0:T(1024)}, u32[]{:S(2)}) copy-start(f32[768]{0:T(1024)} %param.16) | copy-start | bytes 9220
  202.4 4.8 %copy-start.3 = (s32[2,512,1]{1,2,0:T(1,128)S(1)}, s32[2,512,1]{1,2,0:T(1,128)}, u32[]{:S(2)}) copy-start(s32[2,512,1]{1,2,0:T(1,128)} %param.12) | copy-start | bytes 12292
  202.4 46.5 %all-to-all-start.2 = ((bf16[128,2,8,768]{3,2,1,0:T(8,128)(2,1)}), bf16[128,2,8,768]{3,2,1,0:T(8,128)(2,1)S(1)}, u32[]{:S(2)}, u32[]{:S(2)}) async-start(bf16[128,2,8,768]{3,2,1,0:T(8,128)(2,1)} %bitcast.94), calls=%async_computation.2 | async-start | bytes 6291456 | tf_op jit(solution)/shard_map/all_to_all | solution.py:85
Sparse Core Ops, SparseCore 0:
  21.1 67.6 all-gather.1
